TPU v7x, 512 devices: a whole 4x4x16 slice. The times are simulated.
512 devices in a mesh: gx: 32 (over z, x_lo), gy: 16 (over x_hi, y, core).
Axes of the slice: x: 4 (x_hi: 2, x_lo: 2; x = x_hi * 2 + x_lo), y: 4, z: 16, core: 2. Of those that a mesh axis runs over, the one named last changes fastest.
Arguments:
- adjoint_forcing: float32 [4, 6, 1024, 4096], P(None, None, 'gx', 'gy'), may hold values from -6 to 6
- field_mixing: float32 [4, 4], replicated, may hold values from -3 to 3
- time_mixing: float32 [6, 6], replicated, may hold values from -2.5 to 2.5
- kernel_east: float32 [21], replicated, may hold values from 0.1 to 1
- kernel_north: float32 [21], replicated, may hold values from 0.1 to 1
- spatial_modes: bfloat16 [1024, 4096, 256], P('gx', 'gy'), may hold values from -0.00390625 to 0.00390625
- coefficients: float32 [256, 24], P('gy'), may hold values from -6 to 6
Outputs:
- gradient: float32 [256, 24], P('gy')
All inputs are finite; a program needn't handle non-finite values.
Results may differ from a plain program's by a relative error of at most 0.0029.
Values sent between devices are 32-bit elements; how exact they have to be, the bound alone decides.
A program may use at most 64 MiB of HBM per device.

v0:
```python
import jax
import jax.numpy as jnp
from jax import lax
from jax.sharding import PartitionSpec as P


def padded(block, sides, width):
    for axis, dim in sides:
        count = lax.axis_size(axis)
        forward = [(i, i + 1) for i in range(count - 1)]
        backward = [(target, source) for source, target in forward]
        low = lax.ppermute(
            lax.slice_in_dim(block, block.shape[dim] - width, None, axis=dim), axis, forward
        )
        high = lax.ppermute(lax.slice_in_dim(block, 0, width, axis=dim), axis, backward)
        block = jnp.concatenate([low, block, high], axis=dim)
    return block


def smooth_valid(extended, taps, axis, count):
    total = taps[0] * lax.slice_in_dim(extended, 0, count, axis=axis)
    for j in range(1, taps.shape[0]):
        total = total + taps[j] * lax.slice_in_dim(extended, j, j + count, axis=axis)
    return total


def local(
    adjoint_forcing,
    field_mixing,
    time_mixing,
    kernel_east,
    kernel_north,
    spatial_modes,
    coefficients,
):
    fields, levels, width_x, width_y = adjoint_forcing.shape
    reach = (kernel_east.shape[0] - 1) // 2
    mixed = jnp.einsum(
        "gf,st,gsxy->ftxy",
        field_mixing,
        time_mixing,
        adjoint_forcing,
        precision=lax.Precision.HIGHEST,
    )
    wide_x = padded(mixed, (("gx", 2),), reach)
    along_x = smooth_valid(wide_x, kernel_east, 2, width_x)
    wide_y = padded(along_x, (("gy", 3),), reach)
    smoothed = smooth_valid(wide_y, kernel_north, 3, width_y)
    smoothed = smoothed.astype(jnp.bfloat16)
    flat_state = smoothed.reshape(fields * levels, width_x * width_y)
    flat_modes = spatial_modes.reshape(width_x * width_y, spatial_modes.shape[2])
    projection = lax.dot_general(
        flat_modes, flat_state, (((0,), (1,)), ((), ())), preferred_element_type=jnp.float32
    )
    owned = coefficients.shape[0]
    total = lax.psum(projection, ("gx", "gy"))
    mine = lax.dynamic_slice_in_dim(total, lax.axis_index("gy") * owned, owned, 0)
    return coefficients + mine


def solution(mesh):
    in_specs = (P(None, None, "gx", "gy"), P(), P(), P(), P(), P("gx", "gy", None), P("gy", None))
    out_specs = P("gy", None)
    return jax.shard_map(local, mesh=mesh, in_specs=in_specs, out_specs=out_specs, check_vma=False)
```

profile of v0, /device:TPU:1, one launch (start us, length us, event | category | flops | bytes accessed | tf_op | source)
XLA Modules:
  0.0 193.7 jit_solution(18179628404483678090)
XLA Ops:
  0.0 0.0 copy-start
  0.0 3.1 %fusion.118 = f32[6,32,256,4]{2,3,1,0:T(4,128)S(1)} fusion(f32[4,6,32,256]{3,2,1,0:T(8,128)} %param.7, f32[4,4]{1,0:T(4,128)} %param.8), kind=kOutput, calls=%fused_computation.196 | convolution fusion | flops 9437184 | bytes 1572928 | tf_op jit(solution)/shard_map/gf,st,gsxy->ftxy/dot_general | solution.py:38
  3.1 0.0 copy-done
  3.1 0.0 copy-start.2
  3.1 0.0 copy-start.3
  3.1 1.5 convolution_bitcast_fusion
  4.6 0.1 fusion.123
  4.6 4.0 %collective-permute-start = (f32[4,6,10,256]{3,1,0,2:T(8,128)S(1)}, f32[4,6,10,256]{3,1,0,2:T(8,128)S(1)}, u32[]{:S(2)}, u32[]{:S(2)}) collective-permute-start(f32[4,6,10,256]{3,1,0,2:T(8,128)S(1)} %get-tuple-element.7), channel_id=1, source_target_pairs={{0,16},{16,32},{32,48},{48,64},{64,80},{80,96},{96,112},{112,128},... | collective-permute-start | bytes 737288 | tf_op jit(solution)/shard_map/ppermute | solution.py:12
  8.6 1.3 collective-permute-start.1
  9.9 0.0 copy-done.2
  9.9 0.7 fusion.127
  10.6 0.7 fusion.126
  11.3 0.0 copy-done.3
  11.3 0.7 fusion.124
  12.0 0.6 collective-permute-done
  12.6 4.0 %collective-permute-done.1 = f32[4,6,10,256]{3,1,0,2:T(8,128)S(1)} collective-permute-done((f32[4,6,10,256]{3,1,0,2:T(8,128)S(1)}, f32[4,6,10,256]{3,1,0,2:T(8,128)S(1)}, u32[]{:S(2)}, u32[]{:S(2)}) %collective-permute-start.1) | collective-permute-done | bytes 245792 | tf_op jit(solution)/shard_map/ppermute | solution.py:15
  16.5 15.8 %fusion.3 = f32[4,6,32,256]{3,1,0,2:T(8,128)S(1)} fusion(f32[4,6,32,256]{3,1,0,2:T(8,128)S(1)} %convolution_bitcast_fusion, f32[4,6,10,256]{3,1,0,2:T(8,128)S(1)} %collective-permute-done.1, f32[4,6,10,256]{3,1,0,2:T(8,128)S(1)} %collective-permute-done, f32[]{:T(128)} %bitcast.24, f32[]{:T(128)} %bitcast.23, f32[]{:T(128)} %bitcast.22, f32[]{:T(128)} %bitcast.21, ...), kind=kLoop, calls=%fused_computation.77 | loop fusion | flops 11993088 | bytes 2064468 | tf_op jit(solution)/shard_map/add | solution.py:23
  32.4 0.2 fusion.122
  32.6 10.0 %collective-permute-start.2 = (f32[4,6,32,10]{3,1,0,2:T(8,128)S(1)}, f32[4,6,32,10]{3,1,0,2:T(8,128)S(1)}, u32[]{:S(2)}, u32[]{:S(2)}) collective-permute-start(f32[4,6,32,10]{3,1,0,2:T(8,128)S(1)} %get-tuple-element.5), channel_id=1, source_target_pairs={{0,1},{1,2},{2,3},{3,4},{4,5},{5,6},{6,7},{7,8},{8,9},{9,10},{10,1... | collective-permute-start | bytes 92168 | tf_op jit(solution)/shard_map/ppermute | solution.py:12
  42.6 1.9 collective-permute-start.3
  44.6 0.7 fusion.125
  45.2 3.5 %collective-permute-done.2 = f32[4,6,32,10]{3,1,0,2:T(8,128)S(1)} collective-permute-done((f32[4,6,32,10]{3,1,0,2:T(8,128)S(1)}, f32[4,6,32,10]{3,1,0,2:T(8,128)S(1)}, u32[]{:S(2)}, u32[]{:S(2)}) %collective-permute-start.2) | collective-permute-done | bytes 30752 | tf_op jit(solution)/shard_map/ppermute | solution.py:12
  48.7 4.4 %collective-permute-done.3 = f32[4,6,32,10]{3,1,0,2:T(8,128)S(1)} collective-permute-done((f32[4,6,32,10]{3,1,0,2:T(8,128)S(1)}, f32[4,6,32,10]{3,1,0,2:T(8,128)S(1)}, u32[]{:S(2)}, u32[]{:S(2)}) %collective-permute-start.3) | collective-permute-done | bytes 30752 | tf_op jit(solution)/shard_map/ppermute | solution.py:15
  53.1 0.0 copy-start.1
  53.1 22.8 %fusion.60 = bf16[4,6,32,256]{3,1,0,2:T(8,128)(2,1)S(1)} fusion(f32[4,6,32,256]{3,1,0,2:T(8,128)S(1)} %fusion.3, f32[4,6,32,10]{3,1,0,2:T(8,128)S(1)} %collective-permute-done.3, f32[4,6,32,10]{3,1,0,2:T(8,128)S(1)} %collective-permute-done.2, f32[]{:T(128)} %bitcast.44, f32[]{:T(128)} %bitcast.43, f32[]{:T(128)} %bitcast.42, f32[]{:T(128)} %bitcast.41, ...), kind=kLoop, calls=%fused_computation.134 | loop fusion | flops 12189696 | bytes 1241172 | tf_op jit(solution)/shard_map/convert_element_type | solution.py:49
  76.0 0.2 copy.19
  76.2 0.2 copy.26
  76.4 0.0 copy-done.1
  76.4 0.0 copy-start.4
  76.4 1.8 convolution_bitcast_fusion.1
  78.2 114.9 %psum.7 = f32[256,24]{1,0:T(8,128)S(1)} all-reduce(f32[256,24]{1,0:T(8,128)S(1)} %convolution_bitcast_fusion.1), channel_id=1, replica_groups=mesh['gx'=32,'gy'=16] {'gx','gy'}, use_global_device_ids=true, to_apply=%region_0.0 | all-reduce | flops 6144 | bytes 49152 | tf_op jit(solution)/shard_map/psum | solution.py:56
  193.1 0.0 copy-done.4
  193.1 0.6 dynamic-slice_add_fusion
Async XLA Ops:
  0.0 3.1 %copy-start = (f32[6,6]{1,0:T(8,128)S(1)}, f32[6,6]{1,0:T(8,128)}, u32[]{:S(2)}) copy-start(f32[6,6]{1,0:T(8,128)} %param.9) | copy-start | bytes 436
  3.1 6.8 %copy-start.2 = (f32[21]{0:T(128)S(1)}, f32[21]{0:T(128)}, u32[]{:S(2)}) copy-start(f32[21]{0:T(128)} %param.10) | copy-start | bytes 256
  3.1 8.2 %copy-start.3 = (f32[21]{0:T(128)S(1)}, f32[21]{0:T(128)}, u32[]{:S(2)}) copy-start(f32[21]{0:T(128)} %param.11) | copy-start | bytes 256
  4.6 7.9 %collective-permute-start = (f32[4,6,10,256]{3,1,0,2:T(8,128)S(1)}, f32[4,6,10,256]{3,1,0,2:T(8,128)S(1)}, u32[]{:S(2)}, u32[]{:S(2)}) collective-permute-start(f32[4,6,10,256]{3,1,0,2:T(8,128)S(1)} %get-tuple-element.7), channel_id=1, source_target_pairs={{0,16},{16,32},{32,48},{48,64},{64,80},{80,96},{96,112},{112,128},... | collective-permute-start | bytes 737288 | tf_op jit(solution)/shard_map/ppermute | solution.py:12
  8.6 8.0 %collective-permute-start.1 = (f32[4,6,10,256]{3,1,0,2:T(8,128)S(1)}, f32[4,6,10,256]{3,1,0,2:T(8,128)S(1)}, u32[]{:S(2)}, u32[]{:S(2)}) collective-permute-start(f32[4,6,10,256]{3,1,0,2:T(8,128)S(1)} %get-tuple-element.8), channel_id=1, source_target_pairs={{16,0},{32,16},{48,32},{64,48},{80,64},{96,80},{112,96},{128,112},... | collective-permute-start | bytes 737288 | tf_op jit(solution)/shard_map/ppermute | solution.py:15
  32.6 16.2 %collective-permute-start.2 = (f32[4,6,32,10]{3,1,0,2:T(8,128)S(1)}, f32[4,6,32,10]{3,1,0,2:T(8,128)S(1)}, u32[]{:S(2)}, u32[]{:S(2)}) collective-permute-start(f32[4,6,32,10]{3,1,0,2:T(8,128)S(1)} %get-tuple-element.5), channel_id=1, source_target_pairs={{0,1},{1,2},{2,3},{3,4},{4,5},{5,6},{6,7},{7,8},{8,9},{9,10},{10,1... | collective-permute-start | bytes 92168 | tf_op jit(solution)/shard_map/ppermute | solution.py:12
  42.6 10.5 %collective-permute-start.3 = (f32[4,6,32,10]{3,1,0,2:T(8,128)S(1)}, f32[4,6,32,10]{3,1,0,2:T(8,128)S(1)}, u32[]{:S(2)}, u32[]{:S(2)}) collective-permute-start(f32[4,6,32,10]{3,1,0,2:T(8,128)S(1)} %get-tuple-element.6), channel_id=1, source_target_pairs={{1,0},{2,1},{3,2},{4,3},{5,4},{6,5},{7,6},{8,7},{9,8},{10,9},{11,1... | collective-permute-start | bytes 92168 | tf_op jit(solution)/shard_map/ppermute | solution.py:15
  53.1 23.3 %copy-start.1 = (bf16[32,256,256]{2,1,0:T(8,128)(2,1)S(1)}, bf16[32,256,256]{2,1,0:T(8,128)(2,1)}, u32[]{:S(2)}) copy-start(bf16[32,256,256]{2,1,0:T(8,128)(2,1)} %param.12) | copy-start | bytes 12582916
  76.4 116.7 %copy-start.4 = (f32[16,24]{1,0:T(8,128)S(1)}, f32[16,24]{1,0:T(8,128)}, u32[]{:S(2)}) copy-start(f32[16,24]{1,0:T(8,128)} %param.13) | copy-start | bytes 4612
where the time goes:
time: 194 us
  blocking collectives  115 us (59%)
  other arithmetic  39.2 us (20%)
  starting transfers between devices  17.2 us (9%)
  waiting for transfers between devices  12.4 us (6%)
  matrix products  6.28 us (3%)
  local copies, waits for them, and re-layouts  3.52 us (2%)
    psum x1, blocking collectives, local(): total = lax.psum(projection, ('gx', 'gy'))  115 us
    convert_element_type x1, other arithmetic, local(): smoothed = smoothed.astype(jnp.bfloat16)  22.8 us
    add x1, other arithmetic, smooth_valid(): total + taps[j] * lax.slice_in_dim(extended, j, j + count, axis=axis)  15.8 us
    ppermute x2, starting transfers between devices, padded(): lax.ppermute(lax.slice_in_dim(block, block.shape[dim] - width, None, axis...  14 us
    ppermute x2, waiting for transfers between devices, padded(): lax.ppermute(lax.slice_in_dim(block, 0, width, axis=dim), axis, backward)  8.37 us
    dot_general x2, matrix products, local(): jnp.einsum('gf,st,gsxy->ftxy', field_mixing, time_mixing, adjoint_forcing...  4.51 us
    ppermute x2, waiting for transfers between devices, padded(): lax.ppermute(lax.slice_in_dim(block, block.shape[dim] - width, None, axis...  4.06 us
  transfers between devices with their start and end apart: 4, of which 4 were waited for; matrix products, arithmetic and copies ran while one was open for 1% of the time, Pallas kernels for 0%

commit v1 on v0

--- a/solution.py
+++ b/solution.py
@@ -53,7 +53,7 @@
         flat_modes, flat_state, (((0,), (1,)), ((), ())), preferred_element_type=jnp.float32
     )
     owned = coefficients.shape[0]
-    total = lax.psum(projection, ("gx", "gy"))
+    total = lax.psum(lax.psum(projection, "gy"), "gx")
     mine = lax.dynamic_slice_in_dim(total, lax.axis_index("gy") * owned, owned, 0)
     return coefficients + mine
 

time: 194 us -> 280 us (1.44)
  the two profiles are of different devices: /device:TPU:1 before, /device:TPU:4 now
where the time goes in v1:
time: 280 us
  blocking collectives  200 us (71%)
  other arithmetic  39.3 us (14%)
  waiting for transfers between devices  16.5 us (6%)
  starting transfers between devices  13.6 us (5%)
  matrix products  6.27 us (2%)
  local copies, waits for them, and re-layouts  3.52 us (1%)
    psum x2, blocking collectives, local(): total = lax.psum(lax.psum(projection, 'gy'), 'gx')  200 us
    convert_element_type x1, other arithmetic, local(): smoothed = smoothed.astype(jnp.bfloat16)  22.7 us
    add x1, other arithmetic, smooth_valid(): total + taps[j] * lax.slice_in_dim(extended, j, j + count, axis=axis)  15.9 us
    ppermute x2, waiting for transfers between devices, padded(): lax.ppermute(lax.slice_in_dim(block, block.shape[dim] - width, None, axis...  14.8 us
    ppermute x2, starting transfers between devices, padded(): lax.ppermute(lax.slice_in_dim(block, 0, width, axis=dim), axis, backward)  8.55 us
  transfers between devices with their start and end apart: 4, of which 3 were waited for; matrix products, arithmetic and copies ran while one was open for 1% of the time, Pallas kernels for 0%

profile of v1, /device:TPU:4, one launch (start us, length us, event | category | flops | bytes accessed | tf_op | source)
XLA Modules:
  0.0 279.6 jit_solution(9277061477830819370)
XLA Ops:
  0.0 0.0 copy-start
  0.0 3.1 %fusion.118 = f32[6,32,256,4]{2,3,1,0:T(4,128)S(1)} fusion(f32[4,6,32,256]{3,2,1,0:T(8,128)} %param.7, f32[4,4]{1,0:T(4,128)} %param.8), kind=kOutput, calls=%fused_computation.196 | convolution fusion | flops 9437184 | bytes 1572928 | tf_op jit(solution)/shard_map/gf,st,gsxy->ftxy/dot_general | solution.py:38
  3.1 0.0 copy-done
  3.1 0.0 copy-start.2
  3.1 0.0 copy-start.3
  3.1 1.5 convolution_bitcast_fusion
  4.6 0.1 fusion.123
  4.6 3.1 %collective-permute-start = (f32[4,6,10,256]{3,1,0,2:T(8,128)S(1)}, f32[4,6,10,256]{3,1,0,2:T(8,128)S(1)}, u32[]{:S(2)}, u32[]{:S(2)}) collective-permute-start(f32[4,6,10,256]{3,1,0,2:T(8,128)S(1)} %get-tuple-element.7), channel_id=1, source_target_pairs={{0,16},{16,32},{32,48},{48,64},{64,80},{80,96},{96,112},{112,128},... | collective-permute-start | bytes 737288 | tf_op jit(solution)/shard_map/ppermute | solution.py:12
  7.7 1.3 collective-permute-start.1
  9.0 0.0 copy-done.2
  9.1 0.7 fusion.127
  9.7 0.7 fusion.126
  10.4 0.0 copy-done.3
  10.5 0.7 fusion.124
  11.2 10.5 %collective-permute-done = f32[4,6,10,256]{3,1,0,2:T(8,128)S(1)} collective-permute-done((f32[4,6,10,256]{3,1,0,2:T(8,128)S(1)}, f32[4,6,10,256]{3,1,0,2:T(8,128)S(1)}, u32[]{:S(2)}, u32[]{:S(2)}) %collective-permute-start) | collective-permute-done | bytes 245792 | tf_op jit(solution)/shard_map/ppermute | solution.py:12
  21.7 0.0 collective-permute-done.1
  21.7 15.9 %fusion.3 = f32[4,6,32,256]{3,1,0,2:T(8,128)S(1)} fusion(f32[4,6,32,256]{3,1,0,2:T(8,128)S(1)} %convolution_bitcast_fusion, f32[4,6,10,256]{3,1,0,2:T(8,128)S(1)} %collective-permute-done.1, f32[4,6,10,256]{3,1,0,2:T(8,128)S(1)} %collective-permute-done, f32[]{:T(128)} %bitcast.24, f32[]{:T(128)} %bitcast.23, f32[]{:T(128)} %bitcast.22, f32[]{:T(128)} %bitcast.21, ...), kind=kLoop, calls=%fused_computation.77 | loop fusion | flops 11993088 | bytes 2064468 | tf_op jit(solution)/shard_map/add | solution.py:23
  37.7 0.2 fusion.122
  37.9 1.9 collective-permute-start.2
  39.8 7.3 %collective-permute-start.3 = (f32[4,6,32,10]{3,1,0,2:T(8,128)S(1)}, f32[4,6,32,10]{3,1,0,2:T(8,128)S(1)}, u32[]{:S(2)}, u32[]{:S(2)}) collective-permute-start(f32[4,6,32,10]{3,1,0,2:T(8,128)S(1)} %get-tuple-element.6), channel_id=1, source_target_pairs={{1,0},{2,1},{3,2},{4,3},{5,4},{6,5},{7,6},{8,7},{9,8},{10,9},{11,1... | collective-permute-start | bytes 92168 | tf_op jit(solution)/shard_map/ppermute | solution.py:15
  47.1 0.7 fusion.125
  47.7 4.3 %collective-permute-done.2 = f32[4,6,32,10]{3,1,0,2:T(8,128)S(1)} collective-permute-done((f32[4,6,32,10]{3,1,0,2:T(8,128)S(1)}, f32[4,6,32,10]{3,1,0,2:T(8,128)S(1)}, u32[]{:S(2)}, u32[]{:S(2)}) %collective-permute-start.2) | collective-permute-done | bytes 30752 | tf_op jit(solution)/shard_map/ppermute | solution.py:12
  52.0 1.8 collective-permute-done.3
  53.7 0.0 copy-start.1
  53.7 22.7 %fusion.60 = bf16[4,6,32,256]{3,1,0,2:T(8,128)(2,1)S(1)} fusion(f32[4,6,32,256]{3,1,0,2:T(8,128)S(1)} %fusion.3, f32[4,6,32,10]{3,1,0,2:T(8,128)S(1)} %collective-permute-done.3, f32[4,6,32,10]{3,1,0,2:T(8,128)S(1)} %collective-permute-done.2, f32[]{:T(128)} %bitcast.44, f32[]{:T(128)} %bitcast.43, f32[]{:T(128)} %bitcast.42, f32[]{:T(128)} %bitcast.41, ...), kind=kLoop, calls=%fused_computation.134 | loop fusion | flops 12189696 | bytes 1241172 | tf_op jit(solution)/shard_map/convert_element_type | solution.py:49
  76.5 0.2 copy.19
  76.7 0.2 copy.26
  77.0 0.0 copy-done.1
  77.0 0.0 copy-start.4
  77.0 1.8 convolution_bitcast_fusion.1
  78.8 71.2 %psum.14 = f32[256,24]{1,0:T(8,128)S(1)} all-reduce(f32[256,24]{1,0:T(8,128)S(1)} %convolution_bitcast_fusion.1), channel_id=1, replica_groups=mesh['gx'=32,'gy'=16] {'gy'}, use_global_device_ids=true, to_apply=%region_0.0 | all-reduce | flops 6144 | bytes 49152 | tf_op jit(solution)/shard_map/psum | solution.py:56
  149.9 129.0 %psum.15 = f32[256,24]{1,0:T(8,128)S(1)} all-reduce(f32[256,24]{1,0:T(8,128)S(1)} %psum.14), channel_id=1, replica_groups=mesh['gx'=32,'gy'=16] {'gx'}, use_global_device_ids=true, to_apply=%region_1.0 | all-reduce | flops 6144 | bytes 49152 | tf_op jit(solution)/shard_map/psum | solution.py:56
  279.0 0.0 copy-done.4
  279.0 0.6 dynamic-slice_add_fusion
Async XLA Ops:
  0.0 3.1 %copy-start = (f32[6,6]{1,0:T(8,128)S(1)}, f32[6,6]{1,0:T(8,128)}, u32[]{:S(2)}) copy-start(f32[6,6]{1,0:T(8,128)} %param.9) | copy-start | bytes 436
  3.1 6.0 %copy-start.2 = (f32[21]{0:T(128)S(1)}, f32[21]{0:T(128)}, u32[]{:S(2)}) copy-start(f32[21]{0:T(128)} %param.10) | copy-start | bytes 256
  3.1 7.4 %copy-start.3 = (f32[21]{0:T(128)S(1)}, f32[21]{0:T(128)}, u32[]{:S(2)}) copy-start(f32[21]{0:T(128)} %param.11) | copy-start | bytes 256
  4.6 17.1 %collective-permute-start = (f32[4,6,10,256]{3,1,0,2:T(8,128)S(1)}, f32[4,6,10,256]{3,1,0,2:T(8,128)S(1)}, u32[]{:S(2)}, u32[]{:S(2)}) collective-permute-start(f32[4,6,10,256]{3,1,0,2:T(8,128)S(1)} %get-tuple-element.7), channel_id=1, source_target_pairs={{0,16},{16,32},{32,48},{48,64},{64,80},{80,96},{96,112},{112,128},... | collective-permute-start | bytes 737288 | tf_op jit(solution)/shard_map/ppermute | solution.py:12
  7.7 14.0 %collective-permute-start.1 = (f32[4,6,10,256]{3,1,0,2:T(8,128)S(1)}, f32[4,6,10,256]{3,1,0,2:T(8,128)S(1)}, u32[]{:S(2)}, u32[]{:S(2)}) collective-permute-start(f32[4,6,10,256]{3,1,0,2:T(8,128)S(1)} %get-tuple-element.8), channel_id=1, source_target_pairs={{16,0},{32,16},{48,32},{64,48},{80,64},{96,80},{112,96},{128,112},... | collective-permute-start | bytes 737288 | tf_op jit(solution)/shard_map/ppermute | solution.py:15
  37.9 14.1 %collective-permute-start.2 = (f32[4,6,32,10]{3,1,0,2:T(8,128)S(1)}, f32[4,6,32,10]{3,1,0,2:T(8,128)S(1)}, u32[]{:S(2)}, u32[]{:S(2)}) collective-permute-start(f32[4,6,32,10]{3,1,0,2:T(8,128)S(1)} %get-tuple-element.5), channel_id=1, source_target_pairs={{0,1},{1,2},{2,3},{3,4},{4,5},{5,6},{6,7},{7,8},{8,9},{9,10},{10,1... | collective-permute-start | bytes 92168 | tf_op jit(solution)/shard_map/ppermute | solution.py:12
  39.8 13.9 %collective-permute-start.3 = (f32[4,6,32,10]{3,1,0,2:T(8,128)S(1)}, f32[4,6,32,10]{3,1,0,2:T(8,128)S(1)}, u32[]{:S(2)}, u32[]{:S(2)}) collective-permute-start(f32[4,6,32,10]{3,1,0,2:T(8,128)S(1)} %get-tuple-element.6), channel_id=1, source_target_pairs={{1,0},{2,1},{3,2},{4,3},{5,4},{6,5},{7,6},{8,7},{9,8},{10,9},{11,1... | collective-permute-start | bytes 92168 | tf_op jit(solution)/shard_map/ppermute | solution.py:15
  53.7 23.2 %copy-start.1 = (bf16[32,256,256]{2,1,0:T(8,128)(2,1)S(1)}, bf16[32,256,256]{2,1,0:T(8,128)(2,1)}, u32[]{:S(2)}) copy-start(bf16[32,256,256]{2,1,0:T(8,128)(2,1)} %param.12) | copy-start | bytes 12582916
  77.0 202.0 %copy-start.4 = (f32[16,24]{1,0:T(8,128)S(1)}, f32[16,24]{1,0:T(8,128)}, u32[]{:S(2)}) copy-start(f32[16,24]{1,0:T(8,128)} %param.13) | copy-start | bytes 4612
